TPU v7x, 32 devices: a whole 2x2x4 slice. The times are simulated.
32 devices in a mesh: wide: 16 (over z, x, core), narrow: 2 (over y).
Axes of the slice: x: 2, y: 2, z: 4, core: 2. Of those that a mesh axis runs over, the one named last changes fastest.
Arguments:
- query_rows: bfloat16 [640, 6144], P('wide', 'narrow'), may hold values from -30 to 30
- key_rows: bfloat16 [640, 6144], P('wide', 'narrow'), may hold values from -10 to 10
- value_rows: bfloat16 [640, 6144], P('wide', 'narrow'), may hold values from -6 to 6
- mid_grad: bfloat16 [5120, 2048], P(('wide', 'narrow')), may hold values from -6 to 6
- link_weight: bfloat16 [768, 2048], replicated, may hold values from -0.21875 to 0.21875
Outputs:
- query_grad: bfloat16 [640, 6144], P('wide', 'narrow')
- key_grad: bfloat16 [640, 6144], P('wide', 'narrow')
- value_grad: bfloat16 [640, 6144], P('wide', 'narrow')
All inputs are finite; a program needn't handle non-finite values.
Results may differ from a plain program's by a relative error of at most 0.0066.
Values may be sent and summed in bfloat16 or wider, within the bound.
No kernel may reach another device: no remote copies, remote signals or barrier semaphores. Data moves between devices by JAX's collectives and lax.ppermute only.
A program may use at most 64 MiB of HBM per device.

v0:
```python
import math
import jax
import jax.numpy as jnp
from jax import lax
from jax.sharding import PartitionSpec as P

HD = 128
PATCH = 8
lowest = -1e30


def on_device(query_rows, key_rows, value_rows, mid_grad, link_weight):
    groups = lax.axis_size("narrow")
    patches = query_rows.shape[0]
    columns = query_rows.shape[1]
    heads_here = columns // HD
    scaling = 1.0 / math.sqrt(HD)
    local_patches = mid_grad.shape[0] // PATCH
    grouped = mid_grad.reshape(local_patches, groups, PATCH // groups, mid_grad.shape[1])
    moved = jnp.einsum(
        "abcm,pm->abcp",
        lax.all_to_all(grouped, "narrow", split_axis=1, concat_axis=0, tiled=True),
        link_weight,
        preferred_element_type=jnp.float32,
    ).astype(jnp.bfloat16)
    incoming = moved.reshape(patches, columns)
    incoming_heads = incoming.reshape(patches, heads_here, HD)
    query_heads = query_rows.reshape(patches, heads_here, HD)
    key_heads = key_rows.reshape(patches, heads_here, HD)
    value_heads = value_rows.reshape(patches, heads_here, HD)
    own_pos = lax.axis_index("wide") * patches + jnp.arange(patches, dtype=jnp.int32)
    total_rows = patches * lax.axis_size("wide")
    empty_store = jnp.zeros((total_rows, columns), jnp.bfloat16)
    fold_start = (
        jnp.full((heads_here, patches), lowest, jnp.float32),
        jnp.zeros((heads_here, patches), jnp.float32),
        jnp.zeros((heads_here, patches), jnp.float32),
        empty_store,
        empty_store,
    )
    pieces = (
        lax.all_gather(key_rows, "wide", axis=0, tiled=True),
        lax.all_gather(value_rows, "wide", axis=0, tiled=True),
    )
    key_piece, value_piece = pieces
    piece_rows = key_piece.shape[0]
    key_split = key_piece.reshape(piece_rows, heads_here, HD)
    value_split = value_piece.reshape(piece_rows, heads_here, HD)
    piece_pos = jnp.arange(piece_rows, dtype=jnp.int32)
    allowed = piece_pos[None, None, :] <= own_pos[None, :, None]
    scores = (
        jnp.einsum("qhd,khd->hqk", query_heads, key_split, preferred_element_type=jnp.float32)
        * scaling
    )
    scores = jnp.where(allowed, scores, lowest)
    products = jnp.einsum(
        "qhd,khd->hqk", incoming_heads, value_split, preferred_element_type=jnp.float32
    )
    old_max, old_total, old_tilt = fold_start[:3]
    new_max = jnp.maximum(old_max, jnp.max(scores, axis=2))
    expo = jnp.where(allowed, jnp.exp(scores - new_max[:, :, None]), 0.0)
    stats = (new_max, jnp.sum(expo, axis=2), jnp.sum(expo * products, axis=2))
    key_store = pieces[0]
    value_store = pieces[1]
    folded = stats + (key_store, value_store)
    run_max, run_total, run_tilt = (folded[0], folded[1], folded[2])
    log_total = run_max + jnp.log(run_total)
    row_delta = run_tilt / run_total
    key_all = folded[3].reshape(total_rows, heads_here, HD)
    value_all = folded[4].reshape(total_rows, heads_here, HD)
    every_pos = jnp.arange(total_rows, dtype=jnp.int32)
    allowed_q = every_pos[None, None, :] <= own_pos[None, :, None]
    scores_q = (
        jnp.einsum("qhd,khd->hqk", query_heads, key_all, preferred_element_type=jnp.float32)
        * scaling
    )
    products_q = jnp.einsum(
        "qhd,khd->hqk", incoming_heads, value_all, preferred_element_type=jnp.float32
    )
    weights_q = jnp.where(
        allowed_q, jnp.exp(jnp.where(allowed_q, scores_q, lowest) - log_total[:, :, None]), 0.0
    )
    score_grad_q = (weights_q * (products_q - row_delta[:, :, None])).astype(jnp.bfloat16)
    query_accum = jnp.einsum(
        "hqk,khd->qhd", score_grad_q, key_all, preferred_element_type=jnp.float32
    )
    query_grad = (query_accum * scaling).astype(jnp.bfloat16).reshape(patches, columns)
    total_all, delta_all = (
        lax.all_gather(log_total, "wide", axis=1, tiled=True),
        lax.all_gather(row_delta, "wide", axis=1, tiled=True),
    )
    query_piece = lax.all_gather(query_rows, "wide", axis=0, tiled=True)
    grad_piece = lax.all_gather(incoming, "wide", axis=0, tiled=True)
    piece_rows = query_piece.shape[0]
    query_split = query_piece.reshape(piece_rows, heads_here, HD)
    grad_split = grad_piece.reshape(piece_rows, heads_here, HD)
    piece_pos = jnp.arange(piece_rows, dtype=jnp.int32)
    allowed = own_pos[None, None, :] <= piece_pos[None, :, None]
    scores = (
        jnp.einsum("qhd,khd->hqk", query_split, key_heads, preferred_element_type=jnp.float32)
        * scaling
    )
    scores = jnp.where(allowed, scores, lowest)
    products = jnp.einsum(
        "qhd,khd->hqk", grad_split, value_heads, preferred_element_type=jnp.float32
    )
    weights = jnp.where(allowed, jnp.exp(scores - total_all[:, :, None]), 0.0)
    score_grad = (weights * (products - delta_all[:, :, None])).astype(jnp.bfloat16)
    key_accum = jnp.einsum(
        "hqk,qhd->khd", score_grad, query_split, preferred_element_type=jnp.float32
    )
    value_accum = jnp.einsum(
        "hqk,qhd->khd", weights.astype(jnp.bfloat16), grad_split, preferred_element_type=jnp.float32
    )
    key_accum, value_accum = (key_accum, value_accum)
    key_grad = (key_accum * scaling).astype(jnp.bfloat16).reshape(patches, columns)
    value_grad = value_accum.astype(jnp.bfloat16).reshape(patches, columns)
    return (query_grad, key_grad, value_grad)


def solution(mesh):
    in_specs = (
        P("wide", "narrow"),
        P("wide", "narrow"),
        P("wide", "narrow"),
        P(("wide", "narrow"), None),
        P(),
    )
    out_specs = (P("wide", "narrow"), P("wide", "narrow"), P("wide", "narrow"))
    return jax.shard_map(
        on_device, mesh=mesh, in_specs=in_specs, out_specs=out_specs, check_vma=False
    )
```

profile of v0, /device:TPU:0, one launch (start us, length us, event | category | flops | bytes accessed | tf_op | source)
XLA Modules:
  0.0 240.6 jit_solution(15646590345335519802)
XLA Ops:
  9.4 2.3 reshape.125
  11.7 1.4 copy.35
  13.1 13.4 %all_to_all.15 = bf16[20,2,4,2048]{3,2,0,1:T(4,128)(2,1)S(1)} all-to-all(bf16[20,2,4,2048]{3,2,0,1:T(4,128)(2,1)S(1)} %copy.35), channel_id=1, replica_groups=mesh['wide'=16,'narrow'=2] {'narrow'}, dimensions={1} | all-to-all | bytes 1310720 | tf_op jit(solution)/shard_map/all_to_all | solution.py:22
  26.6 1.5 fusion.25
  28.0 0.7 copy.67
  29.0 0.8 copy.37
  29.8 1.7 reshape_reshape.3
  31.5 30.6 %all-gather.7.cloned.1.call-done = bf16[640,3072]{1,0:T(8,128)(2,1)} async-done(((bf16[40,3072]{1,0:T(8,128)(2,1)}), bf16[640,3072]{1,0:T(8,128)(2,1)}) %all-gather.7.cloned.1.call-update) | async-done | bytes 3932176 | tf_op jit(solution)/shard_map/all_gather | solution.py:42
  62.1 6.3 %copy.32 = bf16[640,3072]{0,1:T(8,128)(2,1)} copy(bf16[640,3072]{1,0:T(8,128)(2,1)} %all-gather.7.cloned.1.call-done) | data formatting | bytes 7864320 | tf_op jit(solution)/shard_map/all_gather | solution.py:42
  68.4 43.6 %all-gather.9.cloned.1.call-done = bf16[640,3072]{1,0:T(8,128)(2,1)} async-done(((bf16[40,3072]{1,0:T(8,128)(2,1)}), bf16[640,3072]{1,0:T(8,128)(2,1)}) %all-gather.9.cloned.1.call-update) | async-done | bytes 3932176 | tf_op jit(solution)/shard_map/all_gather | solution.py:43
  112.0 6.2 %copy.38 = bf16[640,3072]{0,1:T(8,128)(2,1)} copy(bf16[640,3072]{1,0:T(8,128)(2,1)} %all-gather.9.cloned.1.call-done) | data formatting | bytes 7864320 | tf_op jit(solution)/shard_map/all_gather | solution.py:43
  118.3 3.3 %fusion.57 = (f32[24,40]{1,0:T(8,128)S(1)}, f32[24,40,640]{2,1,0:T(8,128)S(1)}) fusion(bf16[640,24,128]{0,2,1:T(8,128)(2,1)} %bitcast.76, pred[40,640]{1,0:T(8,128)(4,1)S(1)} %iota_compare_fusion.1, bf16[40,3072]{1,0:T(8,128)(2,1)S(1)} %copy-done.3), kind=kOutput, calls=%fused_computation.62 | convolution fusion | flops 159128640 | bytes 6664960 | tf_op jit(solution)/shard_map/qhd,khd->hqk/dot_general | solution.py:74
  121.8 1.4 fusion.2
  123.9 1.8 fusion.33
  125.7 0.7 copy.94
  126.4 19.6 %all-gather = f32[16,40,24]{1,2,0:T(8,128)S(1)} all-gather(f32[1,40,24]{1,2,0:T(8,128)S(1)} %bitcast.88), channel_id=1, replica_groups=mesh['wide'=16,'narrow'=2] {'wide'}, dimensions={0}, use_global_device_ids=true | all-gather | bytes 65280 | tf_op jit(solution)/shard_map/all_gather | solution.py:89
  146.2 18.5 %all-gather.1 = f32[16,40,24]{1,2,0:T(8,128)S(1)} all-gather(f32[1,40,24]{1,2,0:T(8,128)S(1)} %bitcast.87), channel_id=1, replica_groups=mesh['wide'=16,'narrow'=2] {'wide'}, dimensions={0}, use_global_device_ids=true | all-gather | bytes 65280 | tf_op jit(solution)/shard_map/all_gather | solution.py:90
  164.9 6.4 %copy.43 = bf16[640,3072]{0,1:T(8,128)(2,1)} copy(bf16[640,3072]{1,0:T(8,128)(2,1)} %all-gather.11.cloned.1.call-done) | data formatting | bytes 7864320 | tf_op jit(solution)/shard_map/all_gather | solution.py:92
  171.4 4.5 %fusion.43 = f32[24,640,40]{1,2,0:T(8,128)} fusion(bf16[640,24,128]{0,2,1:T(8,128)(2,1)} %bitcast.78, bf16[40,3072]{1,0:T(8,128)(2,1)S(1)} %copy-done.4), kind=kOutput, calls=%fused_computation.43 | convolution fusion | flops 157286400 | bytes 6635520 | tf_op jit(solution)/shard_map/qhd,khd->hqk/dot_general | solution.py:100
  175.9 37.4 %all-gather.13.cloned.1.call-done = bf16[640,3072]{1,0:T(8,128)(2,1)} async-done(((bf16[40,3072]{1,0:T(8,128)(2,1)}), bf16[640,3072]{1,0:T(8,128)(2,1)}) %all-gather.13.cloned.1.call-update) | async-done | bytes 3932176 | tf_op jit(solution)/shard_map/all_gather | solution.py:93
  213.3 6.3 %copy.48 = bf16[640,3072]{0,1:T(8,128)(2,1)} copy(bf16[640,3072]{1,0:T(8,128)(2,1)} %all-gather.13.cloned.1.call-done) | data formatting | bytes 7864320 | tf_op jit(solution)/shard_map/all_gather | solution.py:93
  219.6 5.3 %fusion.35 = bf16[24,5,8,128]{3,2,1,0:T(8,128)(2,1)} fusion(bf16[640,24,128]{0,2,1:T(8,128)(2,1)} %bitcast.81, f32[24,640,40]{1,2,0:T(8,128)} %fusion.43, f32[24,640]{1,0:T(8,128)S(1)} %bitcast.89, pred[640,40]{0,1:T(8,128)(4,1)S(1)} %iota_compare_fusion), kind=kOutput, calls=%fused_computation.36 | convolution fusion | flops 160481280 | bytes 6722560 | tf_op jit(solution)/shard_map/hqk,qhd->khd/dot_general | solution.py:112
  224.9 7.3 %fusion.34 = bf16[24,5,8,128]{3,2,1,0:T(8,128)(2,1)} fusion(bf16[640,24,128]{0,2,1:T(8,128)(2,1)} %bitcast.79, f32[24,640,40]{1,2,0:T(8,128)} %fusion.43, bf16[640,24,128]{0,2,1:T(8,128)(2,1)} %bitcast.82, f32[24,640]{1,0:T(8,128)S(1)} %bitcast.91, f32[24,640]{1,0:T(8,128)S(1)} %bitcast.90, pred[640,40]{0,1:T(8,128)(4,1)S(1)} %iota_compare_fusion, ...), kind=kOutput, calls=%fused_computation.35 | convolution fusion | flops 319119360 | bytes 10961920 | tf_op jit(solution)/shard_map/hqk,qhd->khd/dot_general | solution.py:109
  232.1 1.9 copy_bitcast_fusion
  (32 shorter events, 3.7 us)
Async XLA Ops:
  7.2 19.4 %copy-start = (bf16[768,2048]{1,0:T(8,128)(2,1)S(1)}, bf16[768,2048]{1,0:T(8,128)(2,1)}, u32[]{:S(2)}) copy-start(bf16[768,2048]{1,0:T(8,128)(2,1)} %param.9) | copy-start | bytes 9437188
  7.2 54.9 %all-gather.7.cloned.1.call-start = ((), (), s32[]{:S(2)}) async-start(), calls=%async_computation.1 | async-start | bytes 4177920 | tf_op jit(solution)/shard_map/all_gather | solution.py:42
  7.9 104.1 %all-gather.9.cloned.1.call-start = ((), (), s32[]{:S(2)}) async-start(), calls=%async_computation.2 | async-start | bytes 4177920 | tf_op jit(solution)/shard_map/all_gather | solution.py:43
  8.7 156.2 %all-gather.11.cloned.1.call-start = ((), (), s32[]{:S(2)}) async-start(), calls=%async_computation.3 | async-start | bytes 4177920 | tf_op jit(solution)/shard_map/all_gather | solution.py:92
  9.4 203.9 %all-gather.13.cloned.1.call-start = ((), (), s32[]{:S(2)}) async-start(), calls=%async_computation.4 | async-start | bytes 4177920 | tf_op jit(solution)/shard_map/all_gather | solution.py:93
  68.4 49.9 %copy-start.3 = (bf16[40,3072]{1,0:T(8,128)(2,1)S(1)}, bf16[40,3072]{1,0:T(8,128)(2,1)}, u32[]{:S(2)}) copy-start(bf16[40,3072]{1,0:T(8,128)(2,1)} %param.5) | copy-start | bytes 737284
  118.3 3.5 %copy-start.2 = (bf16[640,3072]{0,1:T(8,128)(2,1)S(1)}, bf16[640,3072]{0,1:T(8,128)(2,1)}, u32[]{:S(2)}) copy-start(bf16[640,3072]{0,1:T(8,128)(2,1)} %copy.38) | copy-start | bytes 11796484
  118.3 3.5 %copy-start.5 = (bf16[40,24,128]{2,1,0:T(8,128)(2,1)S(1)}, bf16[40,24,128]{2,1,0:T(8,128)(2,1)}, u32[]{:S(2)}) copy-start(bf16[40,24,128]{2,1,0:T(8,128)(2,1)} %reshape_reshape.3) | copy-start | bytes 737284
  121.8 2.1 copy-start.1
  164.9 6.5 %copy-start.4 = (bf16[40,3072]{1,0:T(8,128)(2,1)S(1)}, bf16[40,3072]{1,0:T(8,128)(2,1)}, u32[]{:S(2)}) copy-start(bf16[40,3072]{1,0:T(8,128)(2,1)} %param.6) | copy-start | bytes 737284
  219.6 5.3 %copy-start.6 = (bf16[40,3072]{1,0:T(8,128)(2,1)S(1)}, bf16[40,3072]{1,0:T(8,128)(2,1)}, u32[]{:S(2)}) copy-start(bf16[40,3072]{1,0:T(8,128)(2,1)} %param.7) | copy-start | bytes 737284
Sparse Core Ops, SparseCore 0:
  10.3 51.7 all-gather.6
  64.3 47.6 all-gather.8
  114.3 48.4 all-gather.10
  164.9 48.3 all-gather.12
where the time goes:
time: 241 us
  waiting for transfers between devices  114 us (47%)
  blocking collectives  51.5 us (21%)
  local copies, waits for them, and re-layouts  36.1 us (15%)
  matrix products  25 us (10%)
  between operations  13.9 us (6%)
    all_gather x1, waiting for transfers between devices, on_device(): lax.all_gather(value_rows, 'wide', axis=0, tiled=True)  43.6 us
    all_gather x1, waiting for transfers between devices, on_device(): grad_piece = lax.all_gather(incoming, 'wide', axis=0, tiled=True)  37.4 us
    all_gather x1, waiting for transfers between devices, on_device(): lax.all_gather(key_rows, 'wide', axis=0, tiled=True)  30.6 us
    all_gather x1, blocking collectives, on_device(): lax.all_gather(log_total, 'wide', axis=1, tiled=True)  19.6 us
    all_gather x1, blocking collectives, on_device(): lax.all_gather(row_delta, 'wide', axis=1, tiled=True)  18.5 us
    all_to_all x1, blocking collectives, on_device(): lax.all_to_all(grouped, 'narrow', split_axis=1, concat_axis=0, tiled=True)  13.4 us
    dot_general x1, matrix products, on_device(): jnp.einsum('hqk,qhd->khd', score_grad, query_split, preferred_element_typ...  7.27 us
    all_gather x1, local copies, waits for them, and re-layouts, on_device(): query_piece = lax.all_gather(query_rows, 'wide', axis=0, tiled=True)  6.45 us
  transfers between devices with their start and end apart: 4, of which 3 were waited for; matrix products, arithmetic and copies ran while one was open for 16% of the time, Pallas kernels for 0%

commit v1 on v0

--- a/solution.py
+++ b/solution.py
@@ -7,6 +7,20 @@
 HD = 128
 PATCH = 8
 lowest = -1e30
+
+
+def pass_pieces_all_here(local_x, a_name):
+    carry_out, now = (jax.lax.axis_size(a_name), jax.lax.axis_index(a_name))
+    top, x_new = (local_x, 1)
+    while x_new < carry_out:
+        placed = jax.lax.ppermute(
+            top, axis_name=a_name, perm=[(to_i, to_i ^ x_new) for to_i in range(carry_out)]
+        )
+        left_arr = jnp.concatenate([top, placed], 0)
+        reached = jnp.concatenate([placed, top], 0)
+        top = jnp.where(now & x_new == 0, left_arr, reached)
+        x_new = 2 * x_new
+    return top
 
 
 def on_device(query_rows, key_rows, value_rows, mid_grad, link_weight):
@@ -40,7 +54,7 @@
     )
     pieces = (
         lax.all_gather(key_rows, "wide", axis=0, tiled=True),
-        lax.all_gather(value_rows, "wide", axis=0, tiled=True),
+        pass_pieces_all_here(value_rows, "wide"),
     )
     key_piece, value_piece = pieces
     piece_rows = key_piece.shape[0]

time: 241 us -> 291 us (1.21)
  waiting for transfers between devices: 114 us -> 151 us
  other arithmetic: 0.19 us -> 13.4 us
  blocking collectives: 51.5 us -> 39.1 us
  starting transfers between devices: 0.15 us -> 10.2 us
    ppermute x0 -> x4, waiting for transfers between devices: none -> 139 us  [pass_pieces_all_here(): jax.lax.ppermute(top, axis_name=a_name, perm=[(to_i, to_i ^ x_new) for to...]
    all_gather x1 -> x0, waiting for transfers between devices: 43.6 us -> none  [on_device(): lax.all_gather(value_rows, 'wide', axis=0, tiled=True)]
    all_gather x1, waiting for transfers between devices: 37.4 us -> 0.01 us  [on_device(): grad_piece = lax.all_gather(incoming, 'wide', axis=0, tiled=True)]
    all_gather x1, waiting for transfers between devices: 30.6 us -> 0.01 us  [on_device(): lax.all_gather(key_rows, 'wide', axis=0, tiled=True)]
    all_to_all x1 -> x0, blocking collectives: 13.4 us -> none  [on_device(): lax.all_to_all(grouped, 'narrow', split_axis=1, concat_axis=0, tiled=True)]
    select_n x0 -> x6, other arithmetic: none -> 13.2 us  [pass_pieces_all_here(): top = jnp.where(now & x_new == 0, left_arr, reached)]
    all_to_all x0 -> x1, waiting for transfers between devices: none -> 10.4 us  [on_device(): lax.all_to_all(grouped, 'narrow', split_axis=1, concat_axis=0, tiled=True)]
    concatenate x0 -> x5, local copies, waits for them, and re-layouts: none -> 6.9 us  [pass_pieces_all_here(): left_arr = jnp.concatenate([top, placed], 0)]
  transfers between devices with their start and end apart: 4 -> 8, of which waited for: 3 -> 4; matrix products, arithmetic and copies ran while one was open for 16% -> 19% of each run, Pallas kernels for 0% -> 0%
where the time goes in v1:
time: 291 us
  waiting for transfers between devices  151 us (52%)
  blocking collectives  39.1 us (13%)
  local copies, waits for them, and re-layouts  35.9 us (12%)
  matrix products  27.4 us (9%)
  between operations  13.9 us (5%)
  other arithmetic  13.4 us (5%)
  starting transfers between devices  10.2 us (4%)
    ppermute x4, waiting for transfers between devices, pass_pieces_all_here(): jax.lax.ppermute(top, axis_name=a_name, perm=[(to_i, to_i ^ x_new) for to...  139 us
    all_gather x1, blocking collectives, on_device(): lax.all_gather(log_total, 'wide', axis=1, tiled=True)  20.8 us
    all_gather x1, blocking collectives, on_device(): lax.all_gather(row_delta, 'wide', axis=1, tiled=True)  18.3 us
    select_n x6, other arithmetic, pass_pieces_all_here(): top = jnp.where(now & x_new == 0, left_arr, reached)  13.2 us
    all_to_all x1, waiting for transfers between devices, on_device(): lax.all_to_all(grouped, 'narrow', split_axis=1, concat_axis=0, tiled=True)  10.4 us
    dot_general x1, matrix products, on_device(): jnp.einsum('hqk,qhd->khd', score_grad, query_split, preferred_element_typ...  7.29 us
    concatenate x5, local copies, waits for them, and re-layouts, pass_pieces_all_here(): left_arr = jnp.concatenate([top, placed], 0)  6.9 us
    all_gather x1, local copies, waits for them, and re-layouts, on_device(): query_piece = lax.all_gather(query_rows, 'wide', axis=0, tiled=True)  6.37 us
  transfers between devices with their start and end apart: 8, of which 4 were waited for; matrix products, arithmetic and copies ran while one was open for 19% of the time, Pallas kernels for 0%

profile of v1, /device:TPU:0, one launch (start us, length us, event | category | flops | bytes accessed | tf_op | source)
XLA Modules:
  0.0 290.5 jit_solution(10683717263414463698)
XLA Ops:
  8.7 2.4 reshape.137
  11.0 2.3 copy.53
  13.3 4.3 %all-to-all-start = ((bf16[20,2,4,2048]{3,2,0,1:T(4,128)(2,1)}), bf16[20,2,4,2048]{3,2,0,1:T(4,128)(2,1)}, u32[]{:S(2)}, u32[]{:S(2)}) async-start(bf16[20,2,4,2048]{3,2,0,1:T(4,128)(2,1)} %copy.53), calls=%async_computation | async-start | bytes 1310720 | tf_op jit(solution)/shard_map/all_to_all | solution.py:36
  18.3 10.4 %all-to-all-done = bf16[20,2,4,2048]{3,2,0,1:T(4,128)(2,1)} async-done(((bf16[20,2,4,2048]{3,2,0,1:T(4,128)(2,1)}), bf16[20,2,4,2048]{3,2,0,1:T(4,128)(2,1)}, u32[]{:S(2)}, u32[]{:S(2)}) %all-to-all-start) | async-done | bytes 655392 | tf_op jit(solution)/shard_map/all_to_all | solution.py:36
  28.6 2.5 fusion.32
  32.6 2.0 maximum_select_fusion.7
  36.2 18.5 %collective-permute-done.1 = bf16[80,3072]{1,0:T(8,128)(2,1)} collective-permute-done((bf16[80,3072]{1,0:T(8,128)(2,1)}, bf16[80,3072]{1,0:T(8,128)(2,1)}, u32[]{:S(2)}, u32[]{:S(2)}) %collective-permute-start.1) | collective-permute-done | bytes 491552 | tf_op jit(solution)/shard_map/ppermute | solution.py:16
  54.7 2.7 maximum_select_fusion.5
  58.9 24.6 %collective-permute-done.2 = bf16[160,3072]{1,0:T(8,128)(2,1)} collective-permute-done((bf16[160,3072]{1,0:T(8,128)(2,1)}, bf16[160,3072]{1,0:T(8,128)(2,1)}, u32[]{:S(2)}, u32[]{:S(2)}) %collective-permute-start.2) | collective-permute-done | bytes 983072 | tf_op jit(solution)/shard_map/ppermute | solution.py:16
  83.5 4.2 %maximum_select_fusion.3 = bf16[320,3072]{1,0:T(8,128)(2,1)} fusion(bf16[160,3072]{1,0:T(8,128)(2,1)} %collective-permute-done.2, bf16[160,3072]{1,0:T(8,128)(2,1)} %maximum_select_fusion.5, pred[]{:T(512)S(6)} %eq.13), kind=kLoop, calls=%fused_computation.19 | loop fusion | flops 8847360 | bytes 3932161 | tf_op jit(solution)/shard_map/jit(_where)/select_n | solution.py:21
  87.8 2.1 collective-permute-start.3
  98.7 95.7 %collective-permute-done.3 = bf16[320,3072]{1,0:T(8,128)(2,1)} collective-permute-done((bf16[320,3072]{1,0:T(8,128)(2,1)}, bf16[320,3072]{1,0:T(8,128)(2,1)}, u32[]{:S(2)}, u32[]{:S(2)}) %collective-permute-start.3) | collective-permute-done | bytes 1966112 | tf_op jit(solution)/shard_map/ppermute | solution.py:16
  194.4 3.4 %copy_bitcast_fusion = bf16[320,24,128]{2,0,1:T(8,128)(2,1)} fusion(bf16[320,3072]{1,0:T(8,128)(2,1)} %collective-permute-done.3), kind=kLoop, calls=%fused_computation.17 | loop fusion | bytes 3932160 | tf_op jit(solution)/shard_map/concatenate | solution.py:19
  197.7 6.3 %copy.50 = bf16[640,3072]{0,1:T(8,128)(2,1)} copy(bf16[640,3072]{1,0:T(8,128)(2,1)} %all-gather.6.cloned.1.call-done) | data formatting | bytes 7864320 | tf_op jit(solution)/shard_map/all_gather | solution.py:56
  204.1 3.3 %fusion.60 = (f32[24,40]{1,0:T(8,128)S(1)}, f32[24,40,640]{2,1,0:T(8,128)S(1)}) fusion(bf16[640,24,128]{0,2,1:T(8,128)(2,1)} %bitcast.96, pred[40,640]{1,0:T(8,128)(4,1)S(1)} %iota_compare_fusion.1, bf16[40,3072]{1,0:T(8,128)(2,1)S(1)} %copy-done.4), kind=kOutput, calls=%fused_computation.79 | convolution fusion | flops 159128640 | bytes 6664960 | tf_op jit(solution)/shard_map/qhd,khd->hqk/dot_general | solution.py:88
  207.6 2.8 fusion.9
  213.0 20.8 %all-gather = f32[16,40,24]{1,2,0:T(8,128)S(1)} all-gather(f32[1,40,24]{1,2,0:T(8,128)S(1)} %bitcast.106), channel_id=1, replica_groups=mesh['wide'=16,'narrow'=2] {'wide'}, dimensions={0}, use_global_device_ids=true | all-gather | bytes 65280 | tf_op jit(solution)/shard_map/all_gather | solution.py:103
  234.0 18.3 %all-gather.1 = f32[16,40,24]{1,2,0:T(8,128)S(1)} all-gather(f32[1,40,24]{1,2,0:T(8,128)S(1)} %bitcast.105), channel_id=1, replica_groups=mesh['wide'=16,'narrow'=2] {'wide'}, dimensions={0}, use_global_device_ids=true | all-gather | bytes 65280 | tf_op jit(solution)/shard_map/all_gather | solution.py:104
  252.5 6.4 %copy.69 = bf16[640,3072]{0,1:T(8,128)(2,1)} copy(bf16[640,3072]{1,0:T(8,128)(2,1)} %all-gather.8.cloned.1.call-done) | data formatting | bytes 7864320 | tf_op jit(solution)/shard_map/all_gather | solution.py:106
  258.9 4.3 %fusion.46 = f32[24,640,40]{1,2,0:T(8,128)} fusion(bf16[640,24,128]{0,2,1:T(8,128)(2,1)} %bitcast.98, bf16[40,3072]{1,0:T(8,128)(2,1)S(1)} %copy-done.5), kind=kOutput, calls=%fused_computation.58 | convolution fusion | flops 157286400 | bytes 6635520 | tf_op jit(solution)/shard_map/qhd,khd->hqk/dot_general | solution.py:114
  263.3 6.2 %copy.74 = bf16[640,3072]{0,1:T(8,128)(2,1)} copy(bf16[640,3072]{1,0:T(8,128)(2,1)} %all-gather.10.cloned.1.call-done) | data formatting | bytes 7864320 | tf_op jit(solution)/shard_map/all_gather | solution.py:107
  269.5 5.3 %fusion.42 = bf16[24,5,8,128]{3,2,1,0:T(8,128)(2,1)} fusion(bf16[640,24,128]{0,2,1:T(8,128)(2,1)} %bitcast.100, f32[24,640,40]{1,2,0:T(8,128)} %fusion.46, f32[24,640]{1,0:T(8,128)S(1)} %bitcast.107, pred[640,40]{0,1:T(8,128)(4,1)S(1)} %iota_compare_fusion), kind=kOutput, calls=%fused_computation.47 | convolution fusion | flops 160481280 | bytes 6722560 | tf_op jit(solution)/shard_map/hqk,qhd->khd/dot_general | solution.py:126
  274.8 7.3 %fusion.41 = bf16[24,5,8,128]{3,2,1,0:T(8,128)(2,1)} fusion(bf16[640,24,128]{0,2,1:T(8,128)(2,1)} %bitcast.99, f32[24,640,40]{1,2,0:T(8,128)} %fusion.46, bf16[640,24,128]{0,2,1:T(8,128)(2,1)} %bitcast.101, f32[24,640]{1,0:T(8,128)S(1)} %bitcast.109, f32[24,640]{1,0:T(8,128)S(1)} %bitcast.108, pred[640,40]{0,1:T(8,128)(4,1)S(1)} %iota_compare_fusion, ...), kind=kOutput, calls=%fused_computation.46 | convolution fusion | flops 319119360 | bytes 10961920 | tf_op jit(solution)/shard_map/hqk,qhd->khd/dot_general | solution.py:123
  282.1 1.9 copy_bitcast_fusion.3
  (56 shorter events, 18.6 us)
Async XLA Ops:
  7.2 21.5 %copy-start = (bf16[768,2048]{1,0:T(8,128)(2,1)S(1)}, bf16[768,2048]{1,0:T(8,128)(2,1)}, u32[]{:S(2)}) copy-start(bf16[768,2048]{1,0:T(8,128)(2,1)} %param.9) | copy-start | bytes 9437188
  7.2 10.5 %copy-start.6 = (bf16[40,3072]{1,0:T(8,128)(2,1)S(1)}, bf16[40,3072]{1,0:T(8,128)(2,1)}, u32[]{:S(2)}) copy-start(bf16[40,3072]{1,0:T(8,128)(2,1)} %param.7) | copy-start | bytes 737284
  7.2 190.5 %all-gather.6.cloned.1.call-start = ((), (), s32[]{:S(2)}) async-start(), calls=%async_computation.1 | async-start | bytes 4177920 | tf_op jit(solution)/shard_map/all_gather | solution.py:56
  7.9 244.6 %all-gather.8.cloned.1.call-start = ((), (), s32[]{:S(2)}) async-start(), calls=%async_computation.2 | async-start | bytes 4177920 | tf_op jit(solution)/shard_map/all_gather | solution.py:106
  13.3 15.3 %all-to-all-start = ((bf16[20,2,4,2048]{3,2,0,1:T(4,128)(2,1)}), bf16[20,2,4,2048]{3,2,0,1:T(4,128)(2,1)}, u32[]{:S(2)}, u32[]{:S(2)}) async-start(bf16[20,2,4,2048]{3,2,0,1:T(4,128)(2,1)} %copy.53), calls=%async_computation | async-start | bytes 1310720 | tf_op jit(solution)/shard_map/all_to_all | solution.py:36
  17.6 245.6 %all-gather.10.cloned.1.call-start = ((), (), s32[]{:S(2)}) async-start(), calls=%async_computation.3 | async-start | bytes 4177920 | tf_op jit(solution)/shard_map/all_gather | solution.py:107
  17.7 14.9 %collective-permute-start = (bf16[40,3072]{1,0:T(8,128)(2,1)S(1)}, bf16[40,3072]{1,0:T(8,128)(2,1)}, u32[]{:S(2)}, u32[]{:S(2)}) collective-permute-start(bf16[40,3072]{1,0:T(8,128)(2,1)S(1)} %copy-done.6), channel_id=1, source_target_pairs={{0,2},{2,0},{4,6},{6,4},{8,10},{10,8},{12,14},{14,12},{16,18},{18,... | collective-permute-start | bytes 737288 | tf_op jit(solution)/shard_map/ppermute | solution.py:16
  31.1 0.7 copy-start.8
  34.5 20.2 %collective-permute-start.1 = (bf16[80,3072]{1,0:T(8,128)(2,1)}, bf16[80,3072]{1,0:T(8,128)(2,1)}, u32[]{:S(2)}, u32[]{:S(2)}) collective-permute-start(bf16[80,3072]{1,0:T(8,128)(2,1)} %maximum_select_fusion.7), channel_id=1, source_target_pairs={{0,4},{2,6},{4,0},{6,2},{8,12},{10,14},{12,8},{14,10},{16,20},{18,... | collective-permute-start | bytes 1474568 | tf_op jit(solution)/shard_map/ppermute | solution.py:16
  57.5 26.1 %collective-permute-start.2 = (bf16[160,3072]{1,0:T(8,128)(2,1)}, bf16[160,3072]{1,0:T(8,128)(2,1)}, u32[]{:S(2)}, u32[]{:S(2)}) collective-permute-start(bf16[160,3072]{1,0:T(8,128)(2,1)} %maximum_select_fusion.5), channel_id=1, source_target_pairs={{0,8},{2,10},{4,12},{6,14},{8,0},{10,2},{12,4},{14,6},{16,24},{18,... | collective-permute-start | bytes 2949128 | tf_op jit(solution)/shard_map/ppermute | solution.py:16
  58.9 33.0 %copy-start.9 = (bf16[40,4,768]{2,0,1:T(8,128)(2,1)S(1)}, bf16[40,4,768]{2,0,1:T(8,128)(2,1)}, u32[]{:S(2)}) copy-start(bf16[40,4,768]{2,0,1:T(8,128)(2,1)} %copy-done.8) | copy-start | bytes 737284
  87.8 106.6 %collective-permute-start.3 = (bf16[320,3072]{1,0:T(8,128)(2,1)}, bf16[320,3072]{1,0:T(8,128)(2,1)}, u32[]{:S(2)}, u32[]{:S(2)}) collective-permute-start(bf16[320,3072]{1,0:T(8,128)(2,1)} %maximum_select_fusion.3), channel_id=1, source_target_pairs={{0,16},{2,18},{4,20},{6,22},{8,24},{10,26},{12,28},{14,30},{16,0},... | collective-permute-start | bytes 5898248 | tf_op jit(solution)/shard_map/ppermute | solution.py:16
  197.7 6.3 %copy-start.4 = (bf16[40,3072]{1,0:T(8,128)(2,1)S(1)}, bf16[40,3072]{1,0:T(8,128)(2,1)}, u32[]{:S(2)}) copy-start(bf16[40,3072]{1,0:T(8,128)(2,1)} %param.5) | copy-start | bytes 737284
  204.1 3.4 %copy-start.2 = (bf16[320,24,128]{2,0,1:T(8,128)(2,1)S(1)}, bf16[320,24,128]{2,0,1:T(8,128)(2,1)}, u32[]{:S(2)}) copy-start(bf16[320,24,128]{2,0,1:T(8,128)(2,1)} %maximum_select_fusion.2) | copy-start | bytes 5898244
  204.1 3.5 %copy-start.3 = (bf16[320,24,128]{2,0,1:T(8,128)(2,1)S(1)}, bf16[320,24,128]{2,0,1:T(8,128)(2,1)}, u32[]{:S(2)}) copy-start(bf16[320,24,128]{2,0,1:T(8,128)(2,1)} %copy_bitcast_fusion) | copy-start | bytes 5898244
  204.1 3.5 %copy-start.10 = (bf16[40,24,128]{2,1,0:T(8,128)(2,1)S(1)}, bf16[40,24,128]{2,1,0:T(8,128)(2,1)}, u32[]{:S(2)}) copy-start(bf16[40,24,128]{2,1,0:T(8,128)(2,1)} %reshape_reshape.3) | copy-start | bytes 737284
  207.6 2.9 copy-start.1
  252.5 6.4 %copy-start.5 = (bf16[40,3072]{1,0:T(8,128)(2,1)S(1)}, bf16[40,3072]{1,0:T(8,128)(2,1)}, u32[]{:S(2)}) copy-start(bf16[40,3072]{1,0:T(8,128)(2,1)} %param.6) | copy-start | bytes 737284
  269.5 5.4 %copy-start.7 = (bf16[40,3072]{1,0:T(8,128)(2,1)S(1)}, bf16[40,3072]{1,0:T(8,128)(2,1)}, u32[]{:S(2)}) copy-start(bf16[40,3072]{1,0:T(8,128)(2,1)} %param.7) | copy-start | bytes 737284
Sparse Core Ops, SparseCore 0:
  10.3 59.9 all-gather.5
  72.6 99.4 all-gather.7
  174.9 73.0 all-gather.9
